TPU v7x, 128 devices: a whole 4x4x4 slice. The times are simulated.
128 devices in a mesh: section: 8 (over y, core), tensor: 16 (over z, x).
Axes of the slice: x: 4, y: 4, z: 4, core: 2. Of those that a mesh axis runs over, the one named last changes fastest.
Arguments:
- resid: bfloat16 [64, 4608], P('section', 'tensor'), may hold values from -6 to 6
- pre_gain: float32 [8, 4608], P('section'), may hold values from 0.5 to 1.5
- post_gain: float32 [8, 4608], P('section'), may hold values from 0.5 to 1.5
- w_query: bfloat16 [8, 4608, 4096], P('section', None, 'tensor'), may hold values from -0.09375 to 0.09375
- w_key: bfloat16 [8, 4608, 2048], P('section', None, 'tensor'), may hold values from -0.09375 to 0.09375
- w_value: bfloat16 [8, 4608, 2048], P('section', None, 'tensor'), may hold values from -0.09375 to 0.09375
- w_out: bfloat16 [8, 4096, 4608], P('section', 'tensor'), may hold values from -0.09375 to 0.09375
- key_cache: bfloat16 [8, 64, 16, 64, 128], P('section', None, 'tensor'), may hold values from -6 to 6
- value_cache: bfloat16 [8, 64, 16, 64, 128], P('section', None, 'tensor'), may hold values from -6 to 6
- lengths: int32 [64], replicated, may hold values from 1 to 64, as said below
- concept: int32 [64], replicated, may hold values from 0 to 511
- steer_layer: int32 [64], replicated, may hold values from 0 to 7
- strength: float32 [64], replicated, may hold values from 0.5 to 2
- directions: bfloat16 [512, 4608], P(None, 'tensor'), may hold values from -6 to 6
Outputs:
- final_resid: bfloat16 [64, 4608], P('section', 'tensor')
Inputs may be any that keep to these rules, and one draw needn't show every extreme that they name: `lengths`: some row of every draw has exactly 64.
All inputs are finite; a program needn't handle non-finite values.
Results may differ from a plain program's by a relative error of at most 0.03.
Values may be sent and summed in bfloat16 or wider, within the bound.
No kernel may reach another device: no remote copies, remote signals or barrier semaphores. Data moves between devices by JAX's collectives and lax.ppermute only.
A program may use at most 64 MiB of HBM per device.

v0:
```python
import jax
import jax.numpy as jnp
from jax import lax
from jax.sharding import PartitionSpec as P

D = 4608
HEADS = 32
KVH = 16
HD = 128


epsilon = 1e-06
softcap_limit = 50.0


def from_behind(value, axis, steps):
    count = lax.axis_size(axis)
    pairs = [(source, (source + steps) % count) for source in range(count)]
    return lax.ppermute(value, axis, pairs)


def rotate(vectors, places):
    half_dim = vectors.shape[-1] // 2
    frequency = 10000.0 ** (-(jnp.arange(half_dim, dtype=jnp.float32) * 2.0) / vectors.shape[-1])
    angles = places[:, None, None] * frequency[None, None, :]
    first = vectors[..., :half_dim]
    second = vectors[..., half_dim:]
    cosine = jnp.cos(angles)
    sine = jnp.sin(angles)
    return jnp.concatenate(
        [first * cosine - second * sine, second * cosine + first * sine], axis=-1
    )


def attend(queries, new_keys, new_values, cache_keys, cache_values, row_lengths, scale):
    scores = (
        jnp.einsum("rkgd,rkcd->rkgc", queries, cache_keys, preferred_element_type=jnp.float32)
        * scale
    )
    own_score = (
        jnp.einsum("rkgd,rkd->rkg", queries, new_keys, preferred_element_type=jnp.float32) * scale
    )
    capped = softcap_limit * jnp.tanh(scores / softcap_limit)
    own_capped = softcap_limit * jnp.tanh(own_score / softcap_limit)
    valid = jnp.arange(cache_keys.shape[2], dtype=jnp.int32)[None, :] < row_lengths[:, None]
    weights = jnp.where(valid[:, None, None, :], jnp.exp(capped - softcap_limit), jnp.float32(0.0))
    own_weight = jnp.exp(own_capped - softcap_limit)
    totals = jnp.sum(weights, axis=-1) + own_weight
    probs = (weights / totals[..., None]).astype(jnp.bfloat16)
    own_prob = (own_weight / totals).astype(jnp.bfloat16)
    mixed = jnp.einsum("rkgc,rkcd->rkgd", probs, cache_values, preferred_element_type=jnp.float32)
    return (
        mixed
        + own_prob.astype(jnp.float32)[..., None] * new_values.astype(jnp.float32)[:, :, None, :]
    )


def on_device(
    resid,
    pre_gain,
    post_gain,
    w_query,
    w_key,
    w_value,
    w_out,
    key_cache,
    value_cache,
    lengths,
    concept,
    steer_layer,
    strength,
    directions,
):
    section_count = lax.axis_size("section")
    section_index = lax.axis_index("section")
    tensor_index = lax.axis_index("tensor")
    row_count = resid.shape[0]
    piece_width = resid.shape[1]
    group = HEADS // KVH
    local_kv = key_cache.shape[2]
    local_heads = local_kv * group
    scale = float(D // HEADS) ** (-0.5)
    pre_scale = pre_gain[0]
    post_scale = post_gain[0]
    query_weight = w_query[0]
    key_weight = w_key[0]
    value_weight = w_value[0]
    out_weight = w_out[0]
    layer_keys = key_cache[0]
    layer_values = value_cache[0]
    concept_ids = jnp.arange(directions.shape[0], dtype=jnp.int32)

    def advance(tick, current):
        batch_index = (section_index - tick) % section_count
        start_tick = tick - section_index
        active = (start_tick >= 0) & (start_tick < section_count)
        first_row = batch_index * row_count
        row_lengths = lax.dynamic_slice_in_dim(lengths, first_row, row_count, 0)
        row_concepts = lax.dynamic_slice_in_dim(concept, first_row, row_count, 0)
        row_steer = lax.dynamic_slice_in_dim(steer_layer, first_row, row_count, 0)
        row_strength = lax.dynamic_slice_in_dim(strength, first_row, row_count, 0)
        cache_keys = lax.dynamic_slice_in_dim(layer_keys, first_row, row_count, 0)
        cache_values = lax.dynamic_slice_in_dim(layer_values, first_row, row_count, 0)
        places = row_lengths.astype(jnp.float32)
        features = lax.all_gather(current, "tensor", axis=1, tiled=True)
        values_full = features.astype(jnp.float32)
        normed = (
            values_full
            * lax.rsqrt(jnp.mean(values_full * values_full, axis=-1, keepdims=True) + epsilon)
            * pre_scale
        ).astype(jnp.bfloat16)
        queries = rotate(
            jnp.dot(normed, query_weight, preferred_element_type=jnp.float32).reshape(
                row_count, local_heads, HD
            ),
            places,
        ).astype(jnp.bfloat16)
        new_keys = rotate(
            jnp.dot(normed, key_weight, preferred_element_type=jnp.float32).reshape(
                row_count, local_kv, HD
            ),
            places,
        ).astype(jnp.bfloat16)
        new_values = (
            jnp.dot(normed, value_weight, preferred_element_type=jnp.float32)
            .astype(jnp.bfloat16)
            .reshape(row_count, local_kv, HD)
        )
        mixed = attend(
            queries.reshape(row_count, local_kv, group, HD),
            new_keys,
            new_values,
            cache_keys,
            cache_values,
            row_lengths,
            scale,
        )
        heads_out = mixed.reshape(row_count, local_heads * HD).astype(jnp.bfloat16)
        partial_sum = jnp.dot(heads_out, out_weight, preferred_element_type=jnp.float32)
        summed = lax.psum(partial_sum.astype(jnp.bfloat16), "tensor").astype(jnp.float32)
        post_full = (
            summed
            * lax.rsqrt(jnp.mean(summed * summed, axis=-1, keepdims=True) + epsilon)
            * post_scale
        )
        post = lax.dynamic_slice_in_dim(post_full, tensor_index * piece_width, piece_width, 1)
        one_hot = (row_concepts[:, None] == concept_ids[None, :]).astype(jnp.bfloat16)
        steer_piece = jnp.dot(one_hot, directions, preferred_element_type=jnp.float32)
        steer_gate = row_strength * (row_steer == section_index).astype(jnp.float32)
        new_state = (current.astype(jnp.float32) + post + steer_gate[:, None] * steer_piece).astype(
            jnp.bfloat16
        )
        updated = jnp.where(active, new_state, current)
        return from_behind(updated, "section", 1)

    return lax.fori_loop(0, 2 * section_count, advance, resid)


def solution(mesh):
    placed = (
        P("section", "tensor"),
        P("section", None),
        P("section", None),
        P("section", None, "tensor"),
        P("section", None, "tensor"),
        P("section", None, "tensor"),
        P("section", "tensor", None),
        P("section", None, "tensor", None, None),
        P("section", None, "tensor", None, None),
        P(),
        P(),
        P(),
        P(),
        P(None, "tensor"),
    )
    return jax.shard_map(
        on_device, mesh=mesh, in_specs=placed, out_specs=P("section", "tensor"), check_vma=False
    )
```

profile of v0, /device:TPU:0, one launch (start us, length us, event | category | flops | bytes accessed | tf_op | source)
XLA Modules:
  0.0 1931.9 jit_solution(3018478432236587724)
XLA Ops:
  7.2 1917.6 %while.17 = (s32[]{:T(128)}, bf16[8,288]{1,0:T(8,128)(2,1)S(1)}, s32[]{:T(128)}, s32[64]{0:T(128)}, f32[1,4608]{1,0:T(1,128)}, /*index=5*/bf16[4608,256]{1,0:T(8...) while((s32[]{:T(128)}, bf16[8,288]{1,0:T(8,128)(2,1)S(1)}, ...), condition=%wide.region_5.6_spmd.clone, body=%wide.region_0.5_spmd.clone.sunk | while | flops 59988824 | bytes 20555248 | solution.py:156
  7.3 25.2 %all-gather.3 = bf16[16,288,8]{1,2,0:T(8,128)(2,1)S(1)} all-gather(bf16[1,288,8]{1,2,0:T(8,128)(2,1)S(1)} %bitcast.84), channel_id=1, replica_groups=mesh['section'=8,'tensor'=16] {'tensor'}, dimensions={0}, use_global_device_ids=true | all-gather | bytes 78336 | tf_op jit(solution)/shard_map/while/body/eval_jaxpr/all_gather | solution.py:105
  43.5 80.9 %all-reduce.2.cloned.1.call-done = bf16[8,4608]{1,0:T(8,128)(2,1)} async-done(((bf16[8,4608]{1,0:T(8,128)(2,1)}), bf16[8,4608]{1,0:T(8,128)(2,1)}) %all-reduce.2.cloned.1.call-update) | async-done | bytes 73744 | tf_op jit(solution)/shard_map/while/body/eval_jaxpr/psum | solution.py:140
  130.9 23.1 %all-gather.3 = bf16[16,288,8]{1,2,0:T(8,128)(2,1)S(1)} all-gather(bf16[1,288,8]{1,2,0:T(8,128)(2,1)S(1)} %bitcast.84), channel_id=1, replica_groups=mesh['section'=8,'tensor'=16] {'tensor'}, dimensions={0}, use_global_device_ids=true | all-gather | bytes 78336 | tf_op jit(solution)/shard_map/while/body/eval_jaxpr/all_gather | solution.py:105
  165.1 78.9 %all-reduce.2.cloned.1.call-done = bf16[8,4608]{1,0:T(8,128)(2,1)} async-done(((bf16[8,4608]{1,0:T(8,128)(2,1)}), bf16[8,4608]{1,0:T(8,128)(2,1)}) %all-reduce.2.cloned.1.call-update) | async-done | bytes 73744 | tf_op jit(solution)/shard_map/while/body/eval_jaxpr/psum | solution.py:140
  250.5 23.1 %all-gather.3 = bf16[16,288,8]{1,2,0:T(8,128)(2,1)S(1)} all-gather(bf16[1,288,8]{1,2,0:T(8,128)(2,1)S(1)} %bitcast.84), channel_id=1, replica_groups=mesh['section'=8,'tensor'=16] {'tensor'}, dimensions={0}, use_global_device_ids=true | all-gather | bytes 78336 | tf_op jit(solution)/shard_map/while/body/eval_jaxpr/all_gather | solution.py:105
  284.7 78.9 %all-reduce.2.cloned.1.call-done = bf16[8,4608]{1,0:T(8,128)(2,1)} async-done(((bf16[8,4608]{1,0:T(8,128)(2,1)}), bf16[8,4608]{1,0:T(8,128)(2,1)}) %all-reduce.2.cloned.1.call-update) | async-done | bytes 73744 | tf_op jit(solution)/shard_map/while/body/eval_jaxpr/psum | solution.py:140
  370.1 23.1 %all-gather.3 = bf16[16,288,8]{1,2,0:T(8,128)(2,1)S(1)} all-gather(bf16[1,288,8]{1,2,0:T(8,128)(2,1)S(1)} %bitcast.84), channel_id=1, replica_groups=mesh['section'=8,'tensor'=16] {'tensor'}, dimensions={0}, use_global_device_ids=true | all-gather | bytes 78336 | tf_op jit(solution)/shard_map/while/body/eval_jaxpr/all_gather | solution.py:105
  404.3 78.9 %all-reduce.2.cloned.1.call-done = bf16[8,4608]{1,0:T(8,128)(2,1)} async-done(((bf16[8,4608]{1,0:T(8,128)(2,1)}), bf16[8,4608]{1,0:T(8,128)(2,1)}) %all-reduce.2.cloned.1.call-update) | async-done | bytes 73744 | tf_op jit(solution)/shard_map/while/body/eval_jaxpr/psum | solution.py:140
  489.7 23.1 %all-gather.3 = bf16[16,288,8]{1,2,0:T(8,128)(2,1)S(1)} all-gather(bf16[1,288,8]{1,2,0:T(8,128)(2,1)S(1)} %bitcast.84), channel_id=1, replica_groups=mesh['section'=8,'tensor'=16] {'tensor'}, dimensions={0}, use_global_device_ids=true | all-gather | bytes 78336 | tf_op jit(solution)/shard_map/while/body/eval_jaxpr/all_gather | solution.py:105
  523.9 78.9 %all-reduce.2.cloned.1.call-done = bf16[8,4608]{1,0:T(8,128)(2,1)} async-done(((bf16[8,4608]{1,0:T(8,128)(2,1)}), bf16[8,4608]{1,0:T(8,128)(2,1)}) %all-reduce.2.cloned.1.call-update) | async-done | bytes 73744 | tf_op jit(solution)/shard_map/while/body/eval_jaxpr/psum | solution.py:140
  643.5 78.9 %all-reduce.2.cloned.1.call-done = bf16[8,4608]{1,0:T(8,128)(2,1)} async-done(((bf16[8,4608]{1,0:T(8,128)(2,1)}), bf16[8,4608]{1,0:T(8,128)(2,1)}) %all-reduce.2.cloned.1.call-update) | async-done | bytes 73744 | tf_op jit(solution)/shard_map/while/body/eval_jaxpr/psum | solution.py:140
  763.1 78.9 %all-reduce.2.cloned.1.call-done = bf16[8,4608]{1,0:T(8,128)(2,1)} async-done(((bf16[8,4608]{1,0:T(8,128)(2,1)}), bf16[8,4608]{1,0:T(8,128)(2,1)}) %all-reduce.2.cloned.1.call-update) | async-done | bytes 73744 | tf_op jit(solution)/shard_map/while/body/eval_jaxpr/psum | solution.py:140
  882.7 78.9 %all-reduce.2.cloned.1.call-done = bf16[8,4608]{1,0:T(8,128)(2,1)} async-done(((bf16[8,4608]{1,0:T(8,128)(2,1)}), bf16[8,4608]{1,0:T(8,128)(2,1)}) %all-reduce.2.cloned.1.call-update) | async-done | bytes 73744 | tf_op jit(solution)/shard_map/while/body/eval_jaxpr/psum | solution.py:140
  1002.3 78.9 %all-reduce.2.cloned.1.call-done = bf16[8,4608]{1,0:T(8,128)(2,1)} async-done(((bf16[8,4608]{1,0:T(8,128)(2,1)}), bf16[8,4608]{1,0:T(8,128)(2,1)}) %all-reduce.2.cloned.1.call-update) | async-done | bytes 73744 | tf_op jit(solution)/shard_map/while/body/eval_jaxpr/psum | solution.py:140
  1121.9 78.9 %all-reduce.2.cloned.1.call-done = bf16[8,4608]{1,0:T(8,128)(2,1)} async-done(((bf16[8,4608]{1,0:T(8,128)(2,1)}), bf16[8,4608]{1,0:T(8,128)(2,1)}) %all-reduce.2.cloned.1.call-update) | async-done | bytes 73744 | tf_op jit(solution)/shard_map/while/body/eval_jaxpr/psum | solution.py:140
  1241.5 78.9 %all-reduce.2.cloned.1.call-done = bf16[8,4608]{1,0:T(8,128)(2,1)} async-done(((bf16[8,4608]{1,0:T(8,128)(2,1)}), bf16[8,4608]{1,0:T(8,128)(2,1)}) %all-reduce.2.cloned.1.call-update) | async-done | bytes 73744 | tf_op jit(solution)/shard_map/while/body/eval_jaxpr/psum | solution.py:140
  1326.9 23.1 %all-gather.3 = bf16[16,288,8]{1,2,0:T(8,128)(2,1)S(1)} all-gather(bf16[1,288,8]{1,2,0:T(8,128)(2,1)S(1)} %bitcast.84), channel_id=1, replica_groups=mesh['section'=8,'tensor'=16] {'tensor'}, dimensions={0}, use_global_device_ids=true | all-gather | bytes 78336 | tf_op jit(solution)/shard_map/while/body/eval_jaxpr/all_gather | solution.py:105
  1361.1 78.9 %all-reduce.2.cloned.1.call-done = bf16[8,4608]{1,0:T(8,128)(2,1)} async-done(((bf16[8,4608]{1,0:T(8,128)(2,1)}), bf16[8,4608]{1,0:T(8,128)(2,1)}) %all-reduce.2.cloned.1.call-update) | async-done | bytes 73744 | tf_op jit(solution)/shard_map/while/body/eval_jaxpr/psum | solution.py:140
  1480.7 78.9 %all-reduce.2.cloned.1.call-done = bf16[8,4608]{1,0:T(8,128)(2,1)} async-done(((bf16[8,4608]{1,0:T(8,128)(2,1)}), bf16[8,4608]{1,0:T(8,128)(2,1)}) %all-reduce.2.cloned.1.call-update) | async-done | bytes 73744 | tf_op jit(solution)/shard_map/while/body/eval_jaxpr/psum | solution.py:140
  1566.0 23.1 %all-gather.3 = bf16[16,288,8]{1,2,0:T(8,128)(2,1)S(1)} all-gather(bf16[1,288,8]{1,2,0:T(8,128)(2,1)S(1)} %bitcast.84), channel_id=1, replica_groups=mesh['section'=8,'tensor'=16] {'tensor'}, dimensions={0}, use_global_device_ids=true | all-gather | bytes 78336 | tf_op jit(solution)/shard_map/while/body/eval_jaxpr/all_gather | solution.py:105
  1600.3 78.9 %all-reduce.2.cloned.1.call-done = bf16[8,4608]{1,0:T(8,128)(2,1)} async-done(((bf16[8,4608]{1,0:T(8,128)(2,1)}), bf16[8,4608]{1,0:T(8,128)(2,1)}) %all-reduce.2.cloned.1.call-update) | async-done | bytes 73744 | tf_op jit(solution)/shard_map/while/body/eval_jaxpr/psum | solution.py:140
  1719.9 78.9 %all-reduce.2.cloned.1.call-done = bf16[8,4608]{1,0:T(8,128)(2,1)} async-done(((bf16[8,4608]{1,0:T(8,128)(2,1)}), bf16[8,4608]{1,0:T(8,128)(2,1)}) %all-reduce.2.cloned.1.call-update) | async-done | bytes 73744 | tf_op jit(solution)/shard_map/while/body/eval_jaxpr/psum | solution.py:140
  1839.5 78.9 %all-reduce.2.cloned.1.call-done = bf16[8,4608]{1,0:T(8,128)(2,1)} async-done(((bf16[8,4608]{1,0:T(8,128)(2,1)}), bf16[8,4608]{1,0:T(8,128)(2,1)}) %all-reduce.2.cloned.1.call-update) | async-done | bytes 73744 | tf_op jit(solution)/shard_map/while/body/eval_jaxpr/psum | solution.py:140
  (779 shorter events, 488.3 us)
Async XLA Ops:
  7.2 117.2 %all-reduce.2.cloned.1.call-start = ((), (), s32[]{:S(2)}) async-start(), calls=%async_computation | async-start | bytes 147456 | tf_op jit(solution)/shard_map/while/body/eval_jaxpr/psum | solution.py:140
  126.6 4.3 collective-permute-start
  130.9 113.2 %all-reduce.2.cloned.1.call-start = ((), (), s32[]{:S(2)}) async-start(), calls=%async_computation | async-start | bytes 147456 | tf_op jit(solution)/shard_map/while/body/eval_jaxpr/psum | solution.py:140
  246.2 4.3 collective-permute-start
  250.5 113.2 %all-reduce.2.cloned.1.call-start = ((), (), s32[]{:S(2)}) async-start(), calls=%async_computation | async-start | bytes 147456 | tf_op jit(solution)/shard_map/while/body/eval_jaxpr/psum | solution.py:140
  365.8 4.3 collective-permute-start
  370.1 113.2 %all-reduce.2.cloned.1.call-start = ((), (), s32[]{:S(2)}) async-start(), calls=%async_computation | async-start | bytes 147456 | tf_op jit(solution)/shard_map/while/body/eval_jaxpr/psum | solution.py:140
  489.7 113.2 %all-reduce.2.cloned.1.call-start = ((), (), s32[]{:S(2)}) async-start(), calls=%async_computation | async-start | bytes 147456 | tf_op jit(solution)/shard_map/while/body/eval_jaxpr/psum | solution.py:140
  605.0 4.3 collective-permute-start
  609.2 113.2 %all-reduce.2.cloned.1.call-start = ((), (), s32[]{:S(2)}) async-start(), calls=%async_computation | async-start | bytes 147456 | tf_op jit(solution)/shard_map/while/body/eval_jaxpr/psum | solution.py:140
  728.8 113.2 %all-reduce.2.cloned.1.call-start = ((), (), s32[]{:S(2)}) async-start(), calls=%async_computation | async-start | bytes 147456 | tf_op jit(solution)/shard_map/while/body/eval_jaxpr/psum | solution.py:140
  844.2 4.3 collective-permute-start
  848.4 113.2 %all-reduce.2.cloned.1.call-start = ((), (), s32[]{:S(2)}) async-start(), calls=%async_computation | async-start | bytes 147456 | tf_op jit(solution)/shard_map/while/body/eval_jaxpr/psum | solution.py:140
  968.0 113.2 %all-reduce.2.cloned.1.call-start = ((), (), s32[]{:S(2)}) async-start(), calls=%async_computation | async-start | bytes 147456 | tf_op jit(solution)/shard_map/while/body/eval_jaxpr/psum | solution.py:140
  1083.4 4.3 collective-permute-start
  1087.6 113.2 %all-reduce.2.cloned.1.call-start = ((), (), s32[]{:S(2)}) async-start(), calls=%async_computation | async-start | bytes 147456 | tf_op jit(solution)/shard_map/while/body/eval_jaxpr/psum | solution.py:140
  1207.2 113.2 %all-reduce.2.cloned.1.call-start = ((), (), s32[]{:S(2)}) async-start(), calls=%async_computation | async-start | bytes 147456 | tf_op jit(solution)/shard_map/while/body/eval_jaxpr/psum | solution.py:140
  1326.8 113.2 %all-reduce.2.cloned.1.call-start = ((), (), s32[]{:S(2)}) async-start(), calls=%async_computation | async-start | bytes 147456 | tf_op jit(solution)/shard_map/while/body/eval_jaxpr/psum | solution.py:140
  1446.4 113.2 %all-reduce.2.cloned.1.call-start = ((), (), s32[]{:S(2)}) async-start(), calls=%async_computation | async-start | bytes 147456 | tf_op jit(solution)/shard_map/while/body/eval_jaxpr/psum | solution.py:140
  1566.0 113.2 %all-reduce.2.cloned.1.call-start = ((), (), s32[]{:S(2)}) async-start(), calls=%async_computation | async-start | bytes 147456 | tf_op jit(solution)/shard_map/while/body/eval_jaxpr/psum | solution.py:140
  1681.3 4.3 collective-permute-start
  1685.6 113.2 %all-reduce.2.cloned.1.call-start = ((), (), s32[]{:S(2)}) async-start(), calls=%async_computation | async-start | bytes 147456 | tf_op jit(solution)/shard_map/while/body/eval_jaxpr/psum | solution.py:140
  1805.2 113.2 %all-reduce.2.cloned.1.call-start = ((), (), s32[]{:S(2)}) async-start(), calls=%async_computation | async-start | bytes 147456 | tf_op jit(solution)/shard_map/while/body/eval_jaxpr/psum | solution.py:140
  1920.5 4.3 collective-permute-start
  (120 other events, 2357.6 us)
Sparse Core Ops, SparseCore 0:
  43.3 81.0 all-reduce.1
  164.9 79.0 all-reduce.1
  284.5 79.0 all-reduce.1
  404.1 79.0 all-reduce.1
  523.7 79.0 all-reduce.1
  643.3 79.0 all-reduce.1
  762.9 79.0 all-reduce.1
  882.5 79.0 all-reduce.1
  1002.1 79.0 all-reduce.1
  1121.7 79.0 all-reduce.1
  1241.3 79.0 all-reduce.1
  1360.9 79.0 all-reduce.1
  1480.5 79.0 all-reduce.1
  1600.1 79.0 all-reduce.1
  1719.7 79.0 all-reduce.1
  1839.3 79.0 all-reduce.1
where the time goes:
time: 1940 us; the launch traced here: 1930 us
  waiting for transfers between devices  1330 us (69%)
  blocking collectives  372 us (19%)
  matrix products  146 us (8%)
  other arithmetic  57.5 us (3%)
    psum x16, waiting for transfers between devices, advance(): lax.psum(partial_sum.astype(jnp.bfloat16), 'tensor').astype(jnp.float32)  1260 us
    all_gather x16, blocking collectives, advance(): features = lax.all_gather(current, 'tensor', axis=1, tiled=True)  372 us
    ppermute x16, waiting for transfers between devices, from_behind(): return lax.ppermute(value, axis, pairs)  68 us
  transfers between devices with their start and end apart: 32, of which 32 were waited for; matrix products, arithmetic and copies ran while one was open for 0% of the time, Pallas kernels for 0%

commit v1 on v0

v1 whole, which is shorter than its diff:
```python
import jax
import jax.numpy as jnp
from jax import lax
from jax.experimental import pallas as pl
from jax.experimental.pallas import tpu as pltpu
from jax.sharding import PartitionSpec as P

D = 4608
HEADS = 32
KVH = 16
HD = 128
GROUP = HEADS // KVH
QW = GROUP * HD
CHUNKS = 6
DC = D // CHUNKS
EPS = 1e-06
CAP = 50.0
SCALE = float(D // HEADS) ** (-0.5)
VMEM = pl.BlockSpec(memory_space=pltpu.VMEM)
ANY = pl.BlockSpec(memory_space=pl.ANY)


def turn(v, cos, sin):
    return v * cos + pltpu.roll(v, HD // 2, 1) * sin


def layer_kernel(
    x_ref, pre_ref, cos_ref, sin_ref, len_ref,
    wq_hbm, wk_hbm, wv_hbm, wo_hbm, kc_hbm, vc_hbm,
    o_ref,
    xs, w, wo, kc, vc, ho, wsem, sem,
):
    rows = xs.shape[0]
    ctx = kc.shape[1]
    blocks, per = x_ref.shape[0], x_ref.shape[1]
    copies = []
    for c in range(CHUNKS):
        at = pl.ds(c * DC, DC)
        copies.append([
            pltpu.make_async_copy(wq_hbm.at[at], w.at[at, pl.ds(0, QW)], wsem.at[3 * c]),
            pltpu.make_async_copy(wk_hbm.at[at], w.at[at, pl.ds(QW, HD)], wsem.at[3 * c + 1]),
            pltpu.make_async_copy(wv_hbm.at[at], w.at[at, pl.ds(QW + HD, HD)], wsem.at[3 * c + 2]),
        ])
    kcopy = pltpu.make_async_copy(kc_hbm, kc, sem.at[0])
    vcopy = pltpu.make_async_copy(vc_hbm, vc, sem.at[1])
    ocopy = pltpu.make_async_copy(wo_hbm, wo, sem.at[2])
    for group in copies:
        for copy in group:
            copy.start()
    kcopy.start()
    vcopy.start()
    ocopy.start()

    for b in range(blocks):
        xs[pl.ds(b * per, per), :] = x_ref[b]
    acc = jnp.zeros((rows, QW + 2 * HD), jnp.float32)
    squares = jnp.zeros((rows, 1), jnp.float32)
    for c in range(CHUNKS):
        part = xs[:, pl.ds(c * DC, DC)].astype(jnp.float32)
        squares += jnp.sum(part * part, axis=1, keepdims=True)
        scaled = (part * pre_ref[:, pl.ds(c * DC, DC)]).astype(jnp.bfloat16)
        for copy in copies[c]:
            copy.wait()
        acc += jnp.dot(scaled, w[pl.ds(c * DC, DC), :], preferred_element_type=jnp.float32)
    acc = acc * lax.rsqrt(squares / D + EPS)
    cos, sin = cos_ref[...], sin_ref[...]
    heads = [turn(acc[:, h * HD:(h + 1) * HD], cos, sin).astype(jnp.bfloat16) for h in range(GROUP)]
    new_k = turn(acc[:, QW:QW + HD], cos, sin).astype(jnp.bfloat16).astype(jnp.float32)
    new_v = acc[:, QW + HD:].astype(jnp.bfloat16).astype(jnp.float32)
    kcopy.wait()
    vcopy.wait()
    n = 8
    col = lax.broadcasted_iota(jnp.int32, (GROUP * n, n * ctx), 1)
    row = lax.broadcasted_iota(jnp.int32, (GROUP * n, n * ctx), 0)
    rel = col - (row % n) * ctx
    for g in range(rows // n):
        lo, hi = g * n, (g + 1) * n
        q = jnp.concatenate([h[lo:hi].astype(jnp.float32) for h in heads], axis=0)
        nk = jnp.concatenate([new_k[lo:hi]] * GROUP, axis=0)
        nv = jnp.concatenate([new_v[lo:hi]] * GROUP, axis=0)
        ln = jnp.concatenate([len_ref[lo:hi, :]] * GROUP, axis=0)
        keys = kc[pl.ds(lo, n)].reshape(n * ctx, HD)
        vals = vc[pl.ds(lo, n)].reshape(n * ctx, HD)
        s = lax.dot_general(
            q.astype(jnp.bfloat16), keys, (((1,), (1,)), ((), ())), preferred_element_type=jnp.float32
        )
        own = jnp.sum(q * nk, axis=1, keepdims=True)
        wt = jnp.exp(CAP * jnp.tanh(s * (SCALE / CAP)) - CAP)
        wt = jnp.where((rel >= 0) & (rel < ln), wt, 0.0)
        own_w = jnp.exp(CAP * jnp.tanh(own * (SCALE / CAP)) - CAP)
        total = jnp.sum(wt, axis=1, keepdims=True) + own_w
        probs = (wt / total).astype(jnp.bfloat16)
        own_p = (own_w / total).astype(jnp.bfloat16).astype(jnp.float32)
        mixed = jnp.dot(probs, vals, preferred_element_type=jnp.float32) + own_p * nv
        for h in range(GROUP):
            ho[pl.ds(lo, n), pl.ds(h * HD, HD)] = mixed[h * n:(h + 1) * n]
    ocopy.wait()
    lhs = ho[...].astype(jnp.bfloat16)
    for c in range(CHUNKS):
        at = pl.ds(c * DC, DC)
        out = jnp.dot(lhs, wo[:, at], preferred_element_type=jnp.float32).astype(jnp.bfloat16)
        for b in range(blocks):
            o_ref[b, :, at] = out[b * per:(b + 1) * per]


def layer_call(x, pre, cos, sin, lens, wq, wk, wv, wo, kc, vc):
    rows = kc.shape[0]
    return pl.pallas_call(
        layer_kernel,
        out_shape=jax.ShapeDtypeStruct(x.shape, jnp.bfloat16),
        in_specs=[VMEM] * 5 + [ANY] * 6,
        out_specs=VMEM,
        scratch_shapes=[
            pltpu.VMEM((rows, D), jnp.bfloat16),
            pltpu.VMEM((D, QW + 2 * HD), jnp.bfloat16),
            pltpu.VMEM(wo.shape, jnp.bfloat16),
            pltpu.VMEM(kc.shape, jnp.bfloat16),
            pltpu.VMEM(vc.shape, jnp.bfloat16),
            pltpu.VMEM((rows, QW), jnp.float32),
            pltpu.SemaphoreType.DMA((3 * CHUNKS,)),
            pltpu.SemaphoreType.DMA((3,)),
        ],
        compiler_params=pltpu.CompilerParams(vmem_limit_bytes=32 << 20),
        name="layer",
    )(x, pre, cos, sin, lens, wq, wk, wv, wo, kc, vc)


def combine_kernel(p_ref, x_ref, post_ref, steer_ref, o_ref):
    total = p_ref[0].astype(jnp.float32)
    for b in range(1, p_ref.shape[0]):
        total += p_ref[b].astype(jnp.float32)
    factor = lax.rsqrt(jnp.mean(total * total, axis=1, keepdims=True) + EPS)
    post = total * factor * post_ref[...]
    o_ref[...] = (x_ref[...].astype(jnp.float32) + post + steer_ref[...]).astype(jnp.bfloat16)


def combine_call(parts, x, post, steer):
    return pl.pallas_call(
        combine_kernel,
        out_shape=jax.ShapeDtypeStruct(x.shape, jnp.bfloat16),
        in_specs=[VMEM] * 4,
        out_specs=VMEM,
        compiler_params=pltpu.CompilerParams(vmem_limit_bytes=8 << 20),
        name="combine",
    )(parts, x, post, steer)


def swap(value, axis):
    return lax.all_to_all(value, axis, 0, 0, tiled=True)


def on_device(
    resid, pre_gain, post_gain, w_query, w_key, w_value, w_out, key_cache, value_cache,
    lengths, concept, steer_layer, strength, directions,
):
    sections = lax.axis_size("section")
    lanes = lax.axis_size("tensor")
    section = lax.axis_index("section")
    lane = lax.axis_index("tensor")
    batch, width = resid.shape
    rows = batch * sections
    per = rows // lanes

    half = HD // 2
    frequency = 10000.0 ** (-(jnp.arange(half, dtype=jnp.float32) * 2.0) / HD)
    angles = lengths.astype(jnp.float32)[:, None] * frequency[None, :]
    cosine, sine = jnp.cos(angles), jnp.sin(angles)
    cos = jnp.concatenate([cosine, cosine], axis=1)
    sin = jnp.concatenate([-sine, sine], axis=1)
    lens = lengths[:, None]

    everyone = swap(jnp.broadcast_to(resid[None], (sections, batch, width)), "section")
    one_hot = (concept[:, None] == jnp.arange(directions.shape[0], dtype=jnp.int32)[None, :])
    picked = jnp.dot(one_hot.astype(jnp.bfloat16), directions, preferred_element_type=jnp.float32)
    both = jnp.concatenate(
        [everyone.reshape(lanes, per, 1, width), picked.astype(jnp.bfloat16).reshape(lanes, per, 1, width)],
        axis=2,
    )
    both = swap(both, "tensor").transpose(2, 1, 0, 3).reshape(2, per, D)
    gate = strength * (steer_layer == section).astype(jnp.float32)
    gate = lax.dynamic_slice_in_dim(gate, lane * per, per, 0)
    steer = gate[:, None] * both[1].astype(jnp.float32)
    weights = (w_query[0], w_key[0], w_value[0], w_out[0],
               key_cache.reshape(rows, *key_cache.shape[3:]), value_cache.reshape(rows, *value_cache.shape[3:]))
    onward = [(s * lanes + t, ((s + 1) % sections) * lanes + t) for s in range(sections) for t in range(lanes)]

    def layer(x):
        full = swap(jnp.broadcast_to(x[None], (lanes, per, D)), "tensor")
        parts = layer_call(full, pre_gain, cos, sin, lens, *weights)
        parts = swap(parts, "tensor")
        return combine_call(parts, x, post_gain, steer)

    def step(s, x):
        x = lax.cond(section == s, layer, lambda v: v, x)
        return lax.ppermute(x, ("section", "tensor"), onward)

    x = lax.fori_loop(0, sections, step, both[0])
    pieces = swap(x.reshape(per, lanes, width).transpose(1, 0, 2), "tensor")
    return swap(pieces.reshape(sections, batch, width), "section")[0]


def solution(mesh):
    placed = (
        P("section", "tensor"),
        P("section", None),
        P("section", None),
        P("section", None, "tensor"),
        P("section", None, "tensor"),
        P("section", None, "tensor"),
        P("section", "tensor", None),
        P("section", None, "tensor", None, None),
        P("section", None, "tensor", None, None),
        P(),
        P(),
        P(),
        P(),
        P(None, "tensor"),
    )
    return jax.shard_map(
        on_device, mesh=mesh, in_specs=placed, out_specs=P("section", "tensor"), check_vma=False
    )
```

time: 1940 us -> 328 us (0.17)
  waiting for transfers between devices: 1330 us -> 126 us
  blocking collectives: 372 us -> 46.1 us
  matrix products: 146 us -> 0.88 us
  starting transfers between devices: 0.32 us -> 141 us
  other arithmetic: 57.5 us -> 2.42 us
    psum x16 -> x0, waiting for transfers between devices: 1260 us -> none  [advance(): lax.psum(partial_sum.astype(jnp.bfloat16), 'tensor').astype(jnp.float32)]
    all_gather x16 -> x0, blocking collectives: 372 us -> none  [advance(): features = lax.all_gather(current, 'tensor', axis=1, tiled=True)]
    dot_general x128 -> x1, matrix products: 146 us -> 0.88 us  [on_device(): jnp.dot(one_hot.astype(jnp.bfloat16), directions, preferred_element_type=...]
    ppermute x16 -> x8, starting transfers between devices: 0.29 us -> 129 us  [step(): return lax.ppermute(x, ('section', 'tensor'), onward)]
    ppermute x16 -> x8, waiting for transfers between devices: 68 us -> 116 us  [step(): return lax.ppermute(x, ('section', 'tensor'), onward)]
    all_to_all x0 -> x4, blocking collectives: none -> 46.1 us  [swap(): return lax.all_to_all(value, axis, 0, 0, tiled=True)]
  transfers between devices with their start and end apart: 32 -> 10, of which waited for: 32 -> 10; matrix products, arithmetic and copies ran while one was open for 0% -> 1% of each run, Pallas kernels for 0% -> 0%
where the time goes in v1:
time: 328 us; the launch traced here: 327 us
  starting transfers between devices  141 us (43%)
  waiting for transfers between devices  126 us (38%)
  blocking collectives  46.1 us (14%)
  Pallas kernels  6.8 us (2%)
  local copies, waits for them, and re-layouts  3.55 us (1%)
    ppermute x8, starting transfers between devices, step(): return lax.ppermute(x, ('section', 'tensor'), onward)  129 us
    ppermute x8, waiting for transfers between devices, step(): return lax.ppermute(x, ('section', 'tensor'), onward)  116 us
    all_to_all x4, blocking collectives, swap(): return lax.all_to_all(value, axis, 0, 0, tiled=True)  46.1 us
    all_to_all x2, starting transfers between devices, swap(): return lax.all_to_all(value, axis, 0, 0, tiled=True)  12.5 us
    all_to_all x2, waiting for transfers between devices, swap(): return lax.all_to_all(value, axis, 0, 0, tiled=True)  9.97 us
    pallas_call x1, Pallas kernels, layer_call(): pl.pallas_call(layer_kernel, out_shape=jax.ShapeDtypeStruct(x.shape, jnp....  6.6 us
  transfers between devices with their start and end apart: 10, of which 10 were waited for; matrix products, arithmetic and copies ran while one was open for 1% of the time, Pallas kernels for 0%

profile of v1, /device:TPU:0, one launch (start us, length us, event | category | flops | bytes accessed | tf_op | source)
XLA Modules:
  0.0 327.0 jit_solution(4675721416547068918)
XLA Ops:
  0.0 1.4 broadcast_in_dim.6
  1.4 4.6 %all-to-all-start.2 = ((bf16[8,8,288]{2,1,0:T(8,128)(2,1)}), bf16[8,8,288]{2,1,0:T(8,128)(2,1)S(1)}, u32[]{:S(2)}, u32[]{:S(2)}) async-start(bf16[8,8,288]{2,1,0:T(8,128)(2,1)} %broadcast_in_dim.6), calls=%async_computation.2 | async-start | bytes 98304 | tf_op jit(solution)/shard_map/all_to_all | solution.py:149
  6.6 0.9 convolution_convert_fusion
  9.2 2.2 all-to-all-done.2
  12.2 7.9 %all-to-all-start.3 = ((bf16[16,4,2,288]{3,1,2,0:T(4,128)(2,1)}), bf16[16,4,2,288]{3,1,2,0:T(4,128)(2,1)S(1)}, u32[]{:S(2)}, u32[]{:S(2)}) async-start(bf16[16,4,2,288]{3,1,2,0:T(4,128)(2,1)} %pad_maximum_fusion), calls=%async_computation.3 | async-start | bytes 196608 | tf_op jit(solution)/shard_map/all_to_all | solution.py:149
  20.2 7.7 %all-to-all-done.3 = bf16[16,4,2,288]{3,1,2,0:T(4,128)(2,1)S(1)} async-done(((bf16[16,4,2,288]{3,1,2,0:T(4,128)(2,1)}), bf16[16,4,2,288]{3,1,2,0:T(4,128)(2,1)S(1)}, u32[]{:S(2)}, u32[]{:S(2)}) %all-to-all-start.3) | async-done | bytes 73760 | tf_op jit(solution)/shard_map/all_to_all | solution.py:149
  28.3 279.3 %while.16 = (s32[]{:T(128)}, bf16[4,4608]{1,0:T(4,128)(2,1)S(1)}, s32[]{:T(128)}, f32[1,4608]{1,0:T(1,128)}, f32[64,128]{1,0:T(8,128)S(1)}, /*index=5*/f32[64,12...) while((s32[]{:T(128)}, bf16[4,4608]{1,0:T(4,128)(2,1)S(1)}, ...), condition=%wide.region_3.0_spmd, body=%wide.region_0.0_spmd.sunk | while | flops 4 | bytes 8073587 | solution.py:197
  28.3 34.5 %conditional.2 = (bf16[4,4608]{1,0:T(4,128)(2,1)S(1)}) conditional(s32[]{:T(128)} %convert_element_type.29, bf16[4,4608]{1,0:T(4,128)(2,1)S(1)} %get-tuple-element.502, (bf16[4,4608]{1,0:T(4,128)(2,1)S(1)}, f32[1,4608]{1,0:T(1,128)}, f32[64,128]{1,0:T(8,128)S(1)}, f32[64,128]{1,0:T(8,128)S(1)}, s32[64,1]{1,0:T(8,128)S(1)}, ...), branch_computations={%region_1.0_spmd, %region_2.0_spmd} | conditional | bytes 7852096 | solution.py:194
  28.5 13.8 %all_to_all.28.x_ref = bf16[16,4,4608]{2,1,0:T(4,128)(2,1)S(1)} all-to-all(bf16[16,4,4608]{2,1,0:T(4,128)(2,1)S(1)} %broadcast_in_dim.0), channel_id=1, replica_groups=mesh['section'=8,'tensor'=16] {'tensor'}, dimensions={0} | all-to-all | bytes 1179648 | tf_op jit(solution)/shard_map/while/body/eval_jaxpr/cond/branch_1_fun/all_to_all | solution.py:149
  42.3 6.6 %layer.1 = bf16[16,4,4608]{2,1,0:T(4,128)(2,1)S(1)} custom-call(bf16[16,4,4608]{2,1,0:T(4,128)(2,1)S(1)} %all_to_all.28.x_ref, f32[1,4608]{1,0:T(1,128)} %get-tuple-element.267.pre_ref, f32[64,128]{1,0:T(8,128)S(1)} %get-tuple-element.268.cos_ref, f32[64,128]{1,0:T(8,128)S(1)} %get-tuple-element.269.sin_ref, s32[64,1]{1,0:T(8,128)S(1)} %get-tuple-element.270.len_ref, ...), custom_call_target="tpu_custom_call" | custom-call | tf_op jit(solution)/shard_map/while/body/eval_jaxpr/cond/branch_1_fun/layer/pallas_call | solution.py:108
  48.9 13.7 %all_to_all.29.p_ref = bf16[16,4,4608]{2,1,0:T(4,128)(2,1)S(1)} all-to-all(bf16[16,4,4608]{2,1,0:T(4,128)(2,1)S(1)} %layer.1), channel_id=1, replica_groups=mesh['section'=8,'tensor'=16] {'tensor'}, dimensions={0} | all-to-all | bytes 1179648 | tf_op jit(solution)/shard_map/while/body/eval_jaxpr/cond/branch_1_fun/all_to_all | solution.py:149
  62.8 4.6 %collective-permute-done = bf16[4,4608]{1,0:T(4,128)(2,1)S(1)} collective-permute-done((bf16[4,4608]{1,0:T(4,128)(2,1)S(1)}, bf16[4,4608]{1,0:T(4,128)(2,1)S(1)}, u32[]{:S(2)}, u32[]{:S(2)}) %collective-permute-start) | collective-permute-done | bytes 36896 | tf_op jit(solution)/shard_map/while/body/eval_jaxpr/ppermute | solution.py:195
  67.4 28.2 %collective-permute-start = (bf16[4,4608]{1,0:T(4,128)(2,1)S(1)}, bf16[4,4608]{1,0:T(4,128)(2,1)S(1)}, u32[]{:S(2)}, u32[]{:S(2)}) collective-permute-start(bf16[4,4608]{1,0:T(4,128)(2,1)S(1)} %get-tuple-element.533), channel_id=1, source_target_pairs={{0,16},{1,17},{2,18},{3,19},{4,20},{5,21},{6,22},{7,23},{8,24},{9,... | collective-permute-start | bytes 110600 | tf_op jit(solution)/shard_map/while/body/eval_jaxpr/ppermute | solution.py:195
  96.9 4.2 %collective-permute-done = bf16[4,4608]{1,0:T(4,128)(2,1)S(1)} collective-permute-done((bf16[4,4608]{1,0:T(4,128)(2,1)S(1)}, bf16[4,4608]{1,0:T(4,128)(2,1)S(1)}, u32[]{:S(2)}, u32[]{:S(2)}) %collective-permute-start) | collective-permute-done | bytes 36896 | tf_op jit(solution)/shard_map/while/body/eval_jaxpr/ppermute | solution.py:195
  101.2 33.5 %collective-permute-start = (bf16[4,4608]{1,0:T(4,128)(2,1)S(1)}, bf16[4,4608]{1,0:T(4,128)(2,1)S(1)}, u32[]{:S(2)}, u32[]{:S(2)}) collective-permute-start(bf16[4,4608]{1,0:T(4,128)(2,1)S(1)} %get-tuple-element.533), channel_id=1, source_target_pairs={{0,16},{1,17},{2,18},{3,19},{4,20},{5,21},{6,22},{7,23},{8,24},{9,... | collective-permute-start | bytes 110600 | tf_op jit(solution)/shard_map/while/body/eval_jaxpr/ppermute | solution.py:195
  135.6 2.5 collective-permute-start
  138.2 2.1 collective-permute-done
  140.3 28.2 %collective-permute-start = (bf16[4,4608]{1,0:T(4,128)(2,1)S(1)}, bf16[4,4608]{1,0:T(4,128)(2,1)S(1)}, u32[]{:S(2)}, u32[]{:S(2)}) collective-permute-start(bf16[4,4608]{1,0:T(4,128)(2,1)S(1)} %get-tuple-element.533), channel_id=1, source_target_pairs={{0,16},{1,17},{2,18},{3,19},{4,20},{5,21},{6,22},{7,23},{8,24},{9,... | collective-permute-start | bytes 110600 | tf_op jit(solution)/shard_map/while/body/eval_jaxpr/ppermute | solution.py:195
  169.5 2.5 collective-permute-start
  172.0 2.1 collective-permute-done
  174.1 33.5 %collective-permute-start = (bf16[4,4608]{1,0:T(4,128)(2,1)S(1)}, bf16[4,4608]{1,0:T(4,128)(2,1)S(1)}, u32[]{:S(2)}, u32[]{:S(2)}) collective-permute-start(bf16[4,4608]{1,0:T(4,128)(2,1)S(1)} %get-tuple-element.533), channel_id=1, source_target_pairs={{0,16},{1,17},{2,18},{3,19},{4,20},{5,21},{6,22},{7,23},{8,24},{9,... | collective-permute-start | bytes 110600 | tf_op jit(solution)/shard_map/while/body/eval_jaxpr/ppermute | solution.py:195
  207.6 100.0 %collective-permute-done = bf16[4,4608]{1,0:T(4,128)(2,1)S(1)} collective-permute-done((bf16[4,4608]{1,0:T(4,128)(2,1)S(1)}, bf16[4,4608]{1,0:T(4,128)(2,1)S(1)}, u32[]{:S(2)}, u32[]{:S(2)}) %collective-permute-start) | collective-permute-done | bytes 36896 | tf_op jit(solution)/shard_map/while/body/eval_jaxpr/ppermute | solution.py:195
  307.8 10.7 %all_to_all.30 = bf16[16,4,288]{2,1,0:T(4,128)(2,1)S(1)} all-to-all(bf16[16,4,288]{2,1,0:T(4,128)(2,1)S(1)} %bitcast.28), channel_id=1, replica_groups=mesh['section'=8,'tensor'=16] {'tensor'}, dimensions={0} | all-to-all | bytes 73728 | tf_op jit(solution)/shard_map/all_to_all | solution.py:149
  318.5 7.9 %all_to_all.31 = bf16[8,8,288]{2,1,0:T(8,128)(2,1)S(1)} all-to-all(bf16[8,8,288]{2,1,0:T(8,128)(2,1)S(1)} %reshape.42), channel_id=1, replica_groups=mesh['section'=8,'tensor'=16] {'section'}, dimensions={0} | all-to-all | bytes 73728 | tf_op jit(solution)/shard_map/all_to_all | solution.py:149
  (48 shorter events, 7.8 us)
Async XLA Ops:
  0.0 6.6 %copy-start = (bf16[512,288]{0,1:T(8,128)(2,1)S(1)}, bf16[512,288]{0,1:T(8,128)(2,1)}, u32[]{:S(2)}) copy-start(bf16[512,288]{0,1:T(8,128)(2,1)} %param.31) | copy-start | bytes 884740
  1.4 10.1 %all-to-all-start.2 = ((bf16[8,8,288]{2,1,0:T(8,128)(2,1)}), bf16[8,8,288]{2,1,0:T(8,128)(2,1)S(1)}, u32[]{:S(2)}, u32[]{:S(2)}) async-start(bf16[8,8,288]{2,1,0:T(8,128)(2,1)} %broadcast_in_dim.6), calls=%async_computation.2 | async-start | bytes 98304 | tf_op jit(solution)/shard_map/all_to_all | solution.py:149
  12.2 15.7 %all-to-all-start.3 = ((bf16[16,4,2,288]{3,1,2,0:T(4,128)(2,1)}), bf16[16,4,2,288]{3,1,2,0:T(4,128)(2,1)S(1)}, u32[]{:S(2)}, u32[]{:S(2)}) async-start(bf16[16,4,2,288]{3,1,2,0:T(4,128)(2,1)} %pad_maximum_fusion), calls=%async_computation.3 | async-start | bytes 196608 | tf_op jit(solution)/shard_map/all_to_all | solution.py:149
  28.3 14.0 %copy-start.1 = (bf16[4608,128]{1,0:T(8,128)(2,1)S(1)}, bf16[4608,128]{1,0:T(8,128)(2,1)}, u32[]{:S(2)}) copy-start(bf16[4608,128]{1,0:T(8,128)(2,1)} %get-tuple-element.272.wk_hbm) | copy-start | bytes 3538948 | tf_op jit(solution)/shard_map/while/body/eval_jaxpr/cond
  42.3 20.3 %copy-start.2 = (f32[1,4608]{1,0:T(1,128)S(1)}, f32[1,4608]{1,0:T(1,128)}, u32[]{:S(2)}) copy-start(f32[1,4608]{1,0:T(1,128)} %get-tuple-element.277.post_ref) | copy-start | bytes 55300 | tf_op jit(solution)/shard_map/while/body/eval_jaxpr/cond
  62.8 4.6 %collective-permute-start = (bf16[4,4608]{1,0:T(4,128)(2,1)S(1)}, bf16[4,4608]{1,0:T(4,128)(2,1)S(1)}, u32[]{:S(2)}, u32[]{:S(2)}) collective-permute-start(bf16[4,4608]{1,0:T(4,128)(2,1)S(1)} %get-tuple-element.533), channel_id=1, source_target_pairs={{0,16},{1,17},{2,18},{3,19},{4,20},{5,21},{6,22},{7,23},{8,24},{9,... | collective-permute-start | bytes 110600 | tf_op jit(solution)/shard_map/while/body/eval_jaxpr/ppermute | solution.py:195
  67.4 29.1 %collective-permute-start = (bf16[4,4608]{1,0:T(4,128)(2,1)S(1)}, bf16[4,4608]{1,0:T(4,128)(2,1)S(1)}, u32[]{:S(2)}, u32[]{:S(2)}) collective-permute-start(bf16[4,4608]{1,0:T(4,128)(2,1)S(1)} %get-tuple-element.533), channel_id=1, source_target_pairs={{0,16},{1,17},{2,18},{3,19},{4,20},{5,21},{6,22},{7,23},{8,24},{9,... | collective-permute-start | bytes 110600 | tf_op jit(solution)/shard_map/while/body/eval_jaxpr/ppermute | solution.py:195
  96.6 4.6 %collective-permute-start = (bf16[4,4608]{1,0:T(4,128)(2,1)S(1)}, bf16[4,4608]{1,0:T(4,128)(2,1)S(1)}, u32[]{:S(2)}, u32[]{:S(2)}) collective-permute-start(bf16[4,4608]{1,0:T(4,128)(2,1)S(1)} %get-tuple-element.533), channel_id=1, source_target_pairs={{0,16},{1,17},{2,18},{3,19},{4,20},{5,21},{6,22},{7,23},{8,24},{9,... | collective-permute-start | bytes 110600 | tf_op jit(solution)/shard_map/while/body/eval_jaxpr/ppermute | solution.py:195
  101.2 34.3 %collective-permute-start = (bf16[4,4608]{1,0:T(4,128)(2,1)S(1)}, bf16[4,4608]{1,0:T(4,128)(2,1)S(1)}, u32[]{:S(2)}, u32[]{:S(2)}) collective-permute-start(bf16[4,4608]{1,0:T(4,128)(2,1)S(1)} %get-tuple-element.533), channel_id=1, source_target_pairs={{0,16},{1,17},{2,18},{3,19},{4,20},{5,21},{6,22},{7,23},{8,24},{9,... | collective-permute-start | bytes 110600 | tf_op jit(solution)/shard_map/while/body/eval_jaxpr/ppermute | solution.py:195
  135.6 4.6 %collective-permute-start = (bf16[4,4608]{1,0:T(4,128)(2,1)S(1)}, bf16[4,4608]{1,0:T(4,128)(2,1)S(1)}, u32[]{:S(2)}, u32[]{:S(2)}) collective-permute-start(bf16[4,4608]{1,0:T(4,128)(2,1)S(1)} %get-tuple-element.533), channel_id=1, source_target_pairs={{0,16},{1,17},{2,18},{3,19},{4,20},{5,21},{6,22},{7,23},{8,24},{9,... | collective-permute-start | bytes 110600 | tf_op jit(solution)/shard_map/while/body/eval_jaxpr/ppermute | solution.py:195
  140.3 29.1 %collective-permute-start = (bf16[4,4608]{1,0:T(4,128)(2,1)S(1)}, bf16[4,4608]{1,0:T(4,128)(2,1)S(1)}, u32[]{:S(2)}, u32[]{:S(2)}) collective-permute-start(bf16[4,4608]{1,0:T(4,128)(2,1)S(1)} %get-tuple-element.533), channel_id=1, source_target_pairs={{0,16},{1,17},{2,18},{3,19},{4,20},{5,21},{6,22},{7,23},{8,24},{9,... | collective-permute-start | bytes 110600 | tf_op jit(solution)/shard_map/while/body/eval_jaxpr/ppermute | solution.py:195
  169.5 4.6 %collective-permute-start = (bf16[4,4608]{1,0:T(4,128)(2,1)S(1)}, bf16[4,4608]{1,0:T(4,128)(2,1)S(1)}, u32[]{:S(2)}, u32[]{:S(2)}) collective-permute-start(bf16[4,4608]{1,0:T(4,128)(2,1)S(1)} %get-tuple-element.533), channel_id=1, source_target_pairs={{0,16},{1,17},{2,18},{3,19},{4,20},{5,21},{6,22},{7,23},{8,24},{9,... | collective-permute-start | bytes 110600 | tf_op jit(solution)/shard_map/while/body/eval_jaxpr/ppermute | solution.py:195
  174.1 133.5 %collective-permute-start = (bf16[4,4608]{1,0:T(4,128)(2,1)S(1)}, bf16[4,4608]{1,0:T(4,128)(2,1)S(1)}, u32[]{:S(2)}, u32[]{:S(2)}) collective-permute-start(bf16[4,4608]{1,0:T(4,128)(2,1)S(1)} %get-tuple-element.533), channel_id=1, source_target_pairs={{0,16},{1,17},{2,18},{3,19},{4,20},{5,21},{6,22},{7,23},{8,24},{9,... | collective-permute-start | bytes 110600 | tf_op jit(solution)/shard_map/while/body/eval_jaxpr/ppermute | solution.py:195
